TPU v7x, 256 devices: a whole 4x4x8 slice. The times are simulated.
256 devices in a mesh: dp: 16 (over y_lo, z), fsdp: 16 (over x, y_hi, core).
Axes of the slice: x: 4, y: 4 (y_hi: 2, y_lo: 2; y = y_hi * 2 + y_lo), z: 8, core: 2. Of those that a mesh axis runs over, the one named last changes fastest.
Arguments:
- frames: bfloat16 [256, 256, 1536], P(('dp', 'fsdp')), may hold values from -6 to 6
- cotangent: bfloat16 [256, 256, 1536], P(('dp', 'fsdp')), may hold values from -6 to 6
- lengths: int32 [256], P(('dp', 'fsdp')), may hold values from 64 to 256, as said below
- weight_slots: bfloat16 [2304, 3072], P('fsdp'), may hold values from -0.15625 to 0.15625
- owner_rows: int32 [2304], replicated, may hold values from -1 to 1535, as said below
- gain_in: float32 [1536], replicated, may hold values from 0.5 to 1.5
- gain_mid: float32 [1536], replicated, may hold values from 0.5 to 1.5
- kernel: float32 [32, 1536], replicated, may hold values from -1 to 1
Outputs:
- frame_grads: bfloat16 [256, 256, 1536], P(('dp', 'fsdp'))
- weight_grads: bfloat16 [2304, 3072], P('fsdp')
- gain_in_grad: float32 [1536], replicated
- gain_mid_grad: float32 [1536], replicated
- kernel_grad: float32 [32, 1536], replicated
Inputs may be any that keep to these rules, and one draw needn't show every extreme that they name: `owner_rows`: slots o * 144 to o * 144 + 143 belong to owner o (index o of fsdp): first the rows it holds, then -1. Each of the 1536 rows is named by exactly one slot. An owner holds between 48 and 144 rows, and some owner holds exactly 144. Rows of weight_slots in slots marked -1 are not used. `lengths`: some utterance has all 256 frames in use.
All inputs are finite; a program needn't handle non-finite values.
Results may differ from a plain program's by a relative error of at most 0.02.
Values may be sent and summed in bfloat16 or wider, within the bound.
A program may use at most 192 MiB of HBM per device.

v0:
```python
import jax
import jax.numpy as jnp
from jax import lax
from jax.sharding import PartitionSpec as P

EPSILON = 1e-05


def norm_rows(values, scales):
    row_mean = jnp.mean(values, axis=-1, keepdims=True)
    centred = values - row_mean
    spread = jnp.mean(centred * centred, axis=-1, keepdims=True)
    return centred * lax.rsqrt(spread + EPSILON) * scales


def branch_tail(projected, gain_mid, kernel, frame_keep):
    features = gain_mid.shape[0]
    kernel_taps = kernel.shape[0]
    gated = (
        projected[..., :features]
        * jax.nn.sigmoid(projected[..., features:])
        * frame_keep[..., None]
    )
    length = gated.shape[1]
    left_pad = kernel_taps // 2
    padded = jnp.pad(gated, ((0, 0), (left_pad, kernel_taps - 1 - left_pad), (0, 0)))
    convolved = jnp.zeros_like(gated)
    for offset in range(kernel_taps):
        convolved = convolved + kernel[offset] * padded[:, offset : offset + length, :]
    mixed = norm_rows(convolved, gain_mid)
    return mixed * jax.nn.sigmoid(mixed) * frame_keep[..., None]


def per_device(frames, cotangent, lengths, weight_slots, owner_rows, gain_in, gain_mid, kernel):
    utterances, length, features = frames.shape
    token_rows = utterances * length
    slot_count = owner_rows.shape[0]
    valid_slot = owner_rows >= 0
    safe_rows = jnp.where(valid_slot, owner_rows, 0)
    valid_mask = valid_slot.astype(jnp.bfloat16)
    frame_keep = (jnp.arange(length)[None, :] < lengths[:, None]).astype(jnp.float32)
    frames_wide = frames.astype(jnp.float32)
    normed, head_back = jax.vjp(norm_rows, frames_wide, gain_in)
    normed_flat = normed.astype(jnp.bfloat16).reshape(token_rows, features)
    gathered = lax.all_gather(weight_slots, "fsdp", axis=0, tiled=True)
    inverse = (
        jnp.zeros((features,), jnp.int32)
        .at[jnp.where(valid_slot, owner_rows, features)]
        .set(jnp.arange(slot_count, dtype=jnp.int32), mode="drop")
    )
    weight = jnp.take(gathered, inverse, axis=0)
    projected = jnp.dot(normed_flat, weight, preferred_element_type=jnp.float32)
    projected = projected.reshape(utterances, length, 2 * features)
    cotangent_wide = cotangent.astype(jnp.float32)

    def run_tail(projected_in, mid_scales, taps_in):
        return branch_tail(projected_in, mid_scales, taps_in, frame_keep)

    branch, tail_back = jax.vjp(run_tail, projected, gain_mid, kernel)
    projected_grad, gain_mid_grad, kernel_grad = tail_back(cotangent_wide)
    grad_flat = projected_grad.astype(jnp.bfloat16).reshape(token_rows, 2 * features)
    normed_grad = lax.dot_general(
        grad_flat, weight, (((1,), (1,)), ((), ())), preferred_element_type=jnp.float32
    )
    frames_back, gain_in_grad = head_back(normed_grad.reshape(utterances, length, features))
    frame_grads = (cotangent_wide + frames_back).astype(jnp.bfloat16)
    owned_rows = lax.psum_scatter(
        lax.dot_general(
            jnp.take(normed_flat, safe_rows, axis=1) * valid_mask[None, :],
            grad_flat,
            (((0,), (0,)), ((), ())),
            preferred_element_type=jnp.float32,
        ).astype(jnp.bfloat16),
        "fsdp",
        scatter_dimension=0,
        tiled=True,
    )
    weight_sum = lax.psum(owned_rows, "dp").astype(jnp.float32)
    gain_in_total, gain_mid_total, kernel_total = lax.psum(
        (gain_in_grad, gain_mid_grad, kernel_grad), ("dp", "fsdp")
    )
    weight_grads = weight_sum.astype(jnp.bfloat16)
    return (frame_grads, weight_grads, gain_in_total, gain_mid_total, kernel_total)


def solution(mesh):
    in_specs = (
        P(("dp", "fsdp"), None, None),
        P(("dp", "fsdp"), None, None),
        P(("dp", "fsdp")),
        P("fsdp", None),
        P(),
        P(),
        P(),
        P(),
    )
    out_specs = (P(("dp", "fsdp"), None, None), P("fsdp", None), P(), P(), P())
    return jax.shard_map(
        per_device, mesh=mesh, in_specs=in_specs, out_specs=out_specs, check_vma=False
    )
```

profile of v0, /device:TPU:2, one launch (start us, length us, event | category | flops | bytes accessed | tf_op | source)
XLA Modules:
  0.0 746.2 jit_solution(6646918404065023754)
XLA Ops:
  8.6 1.3 convert_reduce_fusion
  11.7 7.4 gather_fusion.1
  19.1 9.0 %scatter_custom_fusion = s32[1536]{0:T(1024)S(1)} fusion(s32[2304]{0:T(1024)S(1)} %get-tuple-element.117, s32[2304]{0:T(1024)S(1)} %iota.9, s32[]{:T(128)} %constant.48.clone.1), kind=kCustom, calls=%fused_computation.195 | custom fusion | bytes 6148 | tf_op jit(solution)/shard_map/scatter | solution.py:49
  28.7 86.9 %all-gather.2.cloned.1.call-done = bf16[2304,3072]{1,0:T(8,128)(2,1)} async-done(((bf16[144,3072]{1,0:T(8,128)(2,1)}), bf16[2304,3072]{1,0:T(8,128)(2,1)}) %all-gather.2.cloned.1.call-update) | async-done | bytes 14155792 | tf_op jit(solution)/shard_map/all_gather | solution.py:45
  115.7 24.8 %gather_fusion = bf16[1536,3072]{1,0:T(8,128)(2,1)} fusion(bf16[2304,3072]{1,0:T(8,128)(2,1)} %all-gather.2.cloned.1.call-done, s32[2048]{0:T(1024)S(1)} %pad_clamp_fusion.1), kind=kCustom, calls=%fused_computation | custom fusion | bytes 18880512 | tf_op jit(solution)/shard_map/jit(_take)/gather | solution.py:51
  140.5 6.4 convolution_bitcast_fusion
  147.3 1.2 copy-done.2
  148.6 8.2 %fusion.44 = (f32[256]{0:T(256)S(1)}, f32[1,256,1536]{2,1,0:T(8,128)S(1)}) fusion(f32[1536]{0:T(1024)S(1)} %get-tuple-element.41, f32[1536]{0:T(1024)S(1)} %get-tuple-element.71, f32[1536]{0:T(1024)S(1)} %get-tuple-element.72, f32[1536]{0:T(1024)S(1)} %get-tuple-element.42, f32[1536]{0:T(1024)S(1)} %get-tuple-element.43, f32[1536]{0:T(1024)S(1)} %get-tuple-element.44, ...), kind=kLoop, calls=%fused_computation.216 | loop fusion | flops 25165568 | bytes 3343360 | tf_op jit(solution)/shard_map/jvp()/reduce_sum | solution.py:10
  157.9 1.8 multiply_reduce_fusion.32
  160.2 4.2 multiply_reduce_fusion.30
  164.4 9.1 %broadcast_multiply_fusion.31 = (f32[1,256,1536]{2,1,0:T(8,128)}, f32[1,256,1536]{2,1,0:T(8,128)}, f32[1,256,1536]{2,1,0:T(8,128)}, f32[1,256,1536]{2,1,0:T(8,12...) fusion(f32[1536]{0:T(1024)S(1)} %get-tuple-element.41, ...), kind=kLoop, calls=%fused_computation.149 | loop fusion | flops 7077888 | bytes 28417024 | tf_op jit(solution)/shard_map/transpose(jvp())/mul | solution.py:29
  173.5 7.2 broadcast_multiply_fusion
  180.7 14.8 %pad_add_fusion = f32[1,287,1536]{2,1,0:T(8,128)S(1)} fusion(f32[1,256,1536]{2,1,0:T(8,128)} %get-tuple-element.86, f32[1,256,1536]{2,1,0:T(8,128)} %get-tuple-element.87, f32[1,256,1536]{2,1,0:T(8,128)} %get-tuple-element.88, f32[1,256,1536]{2,1,0:T(8,128)} %get-tuple-element.89, f32[1,256,1536]{2,1,0:T(8,128)} %get-tuple-element.90, ...), kind=kLoop, calls=%fused_computation.24 | loop fusion | flops 11020800 | bytes 42657792 | tf_op jit(solution)/shard_map/transpose(jvp())/add_any | solution.py:29
  195.5 4.9 fusion.16
  202.6 7.9 %convolution_convert_fusion = bf16[2304,3072]{1,0:T(8,128)(2,1)} fusion(bf16[2304,256]{1,0:T(8,128)(2,1)S(1)} %copy-done.7, pred[2304]{0:T(1024)(128)(4,1)S(1)} %get-tuple-element.115, bf16[2304]{0:T(1024)(128)(2,1)S(1)} %get-tuple-element.114, f32[1,256,1536]{2,1,0:T(8,128)S(1)} %fusion.40, f32[1,256,1536]{2,1,0:T(8,128)S(1)} %get-tuple-element.75), kind=kOutput, calls=%fused_computation.3 | convolution fusion | flops 3633709056 | bytes 18488064 | tf_op jit(solution)/shard_map/dot_general | solution.py:68
  211.2 5.0 multiply_reduce_fusion.31
  216.5 1.0 pad_add_fusion.7
  217.5 8.3 %fusion.15 = (f32[256]{0:T(256)S(1)}, f32[256,1536]{1,0:T(8,128)S(1)}) fusion(bf16[1,256,1536]{2,1,0:T(8,128)(2,1)} %param.8, f32[1536]{0:T(1024)S(1)} %copy-done.12, f32[256]{0:T(256)S(1)} %copy-done.19, bf16[1536,3072]{1,0:T(8,128)(2,1)} %gather_fusion, pred[1536]{0:T(1024)(128)(4,1)S(1)} %copy-done.27, f32[1,256,1536]{2,1,0:T(8,128)} %copy-done.6, ...), kind=kOutput, calls=%fused_computation.62 | convolution fusion | flops 2424176384 | bytes 14951936 | tf_op jit(solution)/shard_map/dot_general | solution.py:62
  225.9 120.1 %reduce-scatter.2.cloned.1.call-done = bf16[144,3072]{1,0:T(8,128)(2,1)} async-done(((bf16[2304,3072]{1,0:T(8,128)(2,1)}), bf16[144,3072]{1,0:T(8,128)(2,1)}) %reduce-scatter.2.cloned.1.call-update) | async-done | bytes 884752 | tf_op jit(solution)/shard_map/reduce_scatter | solution.py:67
  346.9 74.4 %all-reduce.67 = (f32[1536]{0:T(1024)}, f32[1536]{0:T(1024)}) all-reduce(f32[1536]{0:T(1024)S(1)} %get-tuple-element.39, f32[1536]{0:T(1024)S(1)} %copy-done.15), channel_id=1, replica_groups=mesh['dp'=16,'fsdp'=16] {'dp','fsdp'}, use_global_device_ids=true, to_apply=%region_12.13 | all-reduce | flops 3072 | bytes 24576 | tf_op jit(solution)/shard_map/psum | solution.py:79
  421.3 1.5 fusion.13
  422.8 175.4 %all-reduce.73.cloned.1.call-done = f32[32,1536]{1,0:T(8,128)} async-done(((f32[32,1536]{1,0:T(8,128)}), f32[32,1536]{1,0:T(8,128)}) %all-reduce.73.cloned.1.call-update) | async-done | bytes 196624 | tf_op jit(solution)/shard_map/psum | solution.py:79
  598.2 138.6 %all-reduce.71.cloned.1.call-done = bf16[144,3072]{1,0:T(8,128)(2,1)} async-done(((bf16[144,3072]{1,0:T(8,128)(2,1)}), bf16[144,3072]{1,0:T(8,128)(2,1)}) %all-reduce.71.cloned.1.call-update) | async-done | bytes 884752 | tf_op jit(solution)/shard_map/psum | solution.py:78
  736.8 2.1 copy.17
  (122 shorter events, 9.4 us)
Async XLA Ops:
  7.2 2.8 copy-start
  7.2 3.7 copy-start.12
  7.2 108.5 %all-gather.2.cloned.1.call-start = ((), (), s32[]{:S(2)}) async-start(), calls=%async_computation.1 | async-start | bytes 15040512 | tf_op jit(solution)/shard_map/all_gather | solution.py:45
  7.9 338.1 %reduce-scatter.2.cloned.1.call-start = ((), (), s32[]{:S(2)}) async-start(), calls=%async_computation.2 | async-start | bytes 15040512 | tf_op jit(solution)/shard_map/reduce_scatter | solution.py:67
  10.0 1.6 copy-start.18
  11.7 16.5 %copy-start.11 = (f32[32,1536]{1,0:T(8,128)S(1)}, f32[32,1536]{1,0:T(8,128)}, u32[]{:S(2)}) copy-start(f32[32,1536]{1,0:T(8,128)} %param.15) | copy-start | bytes 589828
  28.1 129.0 %copy-start.22 = (f32[256]{0:T(256)}, f32[256]{0:T(256)S(1)}, u32[]{:S(2)}) copy-start(f32[256]{0:T(256)S(1)} %compare_convert_fusion.1) | copy-start | bytes 3076
  28.7 111.8 %copy-start.26 = (pred[1536]{0:T(1024)(128)(4,1)}, pred[1536]{0:T(1024)(128)(4,1)S(1)}, u32[]{:S(2)}) copy-start(pred[1536]{0:T(1024)(128)(4,1)S(1)} %compare_and_fusion.1) | copy-start | bytes 4612
  146.9 1.7 copy-start.2
  160.2 13.3 %copy-start.16 = (f32[256]{0:T(256)}, f32[256]{0:T(256)S(1)}, u32[]{:S(2)}) copy-start(f32[256]{0:T(256)S(1)} %negate_multiply_fusion.1) | copy-start | bytes 3076
  180.7 14.8 %copy-start.3 = (f32[1,256,3072]{2,1,0:T(8,128)S(1)}, f32[1,256,3072]{2,1,0:T(8,128)}, u32[]{:S(2)}) copy-start(f32[1,256,3072]{2,1,0:T(8,128)} %copy-done.2) | copy-start | bytes 9437188
  180.7 14.8 %copy-start.5 = (f32[1,256,1536]{2,1,0:T(8,128)S(1)}, f32[1,256,1536]{2,1,0:T(8,128)}, u32[]{:S(2)}) copy-start(f32[1,256,1536]{2,1,0:T(8,128)} %get-tuple-element.85) | copy-start | bytes 4718596
  180.7 14.8 %copy-start.23 = (f32[256]{0:T(256)S(1)}, f32[256]{0:T(256)}, u32[]{:S(2)}) copy-start(f32[256]{0:T(256)} %copy-done.22) | copy-start | bytes 3076
  200.4 1.2 copy-start.4
  200.5 2.1 copy-start.7
  210.6 387.6 %all-reduce.73.cloned.1.call-start = ((), (), s32[]{:S(2)}) async-start(), calls=%async_computation.4 | async-start | bytes 393216 | tf_op jit(solution)/shard_map/psum | solution.py:79
  211.2 6.3 copy-start.19
  211.2 6.3 copy-start.27
  217.5 8.4 %copy-start.25 = (f32[256]{0:T(256)S(1)}, f32[256]{0:T(256)}, u32[]{:S(2)}) copy-start(f32[256]{0:T(256)} %copy-done.24) | copy-start | bytes 3076
  217.5 128.5 %copy-start.21 = (f32[256]{0:T(256)S(1)}, f32[256]{0:T(256)}, u32[]{:S(2)}) copy-start(f32[256]{0:T(256)} %copy-done.20) | copy-start | bytes 3076
  225.8 120.2 %copy-start.1 = (bf16[1,256,1536]{2,1,0:T(8,128)(2,1)S(1)}, bf16[1,256,1536]{2,1,0:T(8,128)(2,1)}, u32[]{:S(2)}) copy-start(bf16[1,256,1536]{2,1,0:T(8,128)(2,1)} %param.8) | copy-start | bytes 2359300
  225.9 510.9 %all-reduce.71.cloned.1.call-start = ((), (), s32[]{:S(2)}) async-start(), calls=%async_computation.3 | async-start | bytes 1769472 | tf_op jit(solution)/shard_map/psum | solution.py:78
  346.0 75.3 %copy-start.9 = (bf16[1,256,1536]{2,1,0:T(8,128)(2,1)S(1)}, bf16[1,256,1536]{2,1,0:T(8,128)(2,1)}, u32[]{:S(2)}) copy-start(bf16[1,256,1536]{2,1,0:T(8,128)(2,1)} %param.9) | copy-start | bytes 2359300
  598.2 140.8 %copy-start.10 = (f32[32,1536]{1,0:T(8,128)S(1)}, f32[32,1536]{1,0:T(8,128)}, u32[]{:S(2)}) copy-start(f32[32,1536]{1,0:T(8,128)} %all-reduce.73.cloned.1.call-done) | copy-start | bytes 589828
  (8 other events, 6.9 us)
Sparse Core Ops, SparseCore 0:
  10.7 104.8 all-gather.1
  210.7 135.3 reduce-scatter.1
  353.0 245.1 all-reduce.72
  600.9 135.8 all-reduce.70
where the time goes:
time: 747 us; the launch traced here: 746 us
  waiting for transfers between devices  522 us (70%)
  blocking collectives  74.4 us (10%)
  other arithmetic  62.2 us (8%)
  local copies, waits for them, and re-layouts  49.9 us (7%)
  matrix products  22.6 us (3%)
  between operations  15.1 us (2%)
    psum x1, waiting for transfers between devices, per_device(): lax.psum((gain_in_grad, gain_mid_grad, kernel_grad), ('dp', 'fsdp'))  175 us
    psum x1, waiting for transfers between devices, per_device(): weight_sum = lax.psum(owned_rows, 'dp').astype(jnp.float32)  139 us
    reduce_scatter x1, waiting for transfers between devices, per_device(): lax.psum_scatter(lax.dot_general(jnp.take(normed_flat, safe_rows, axis=1)...  120 us
    all_gather x1, waiting for transfers between devices, per_device(): gathered = lax.all_gather(weight_slots, 'fsdp', axis=0, tiled=True)  86.9 us
    psum x1, blocking collectives, per_device(): lax.psum((gain_in_grad, gain_mid_grad, kernel_grad), ('dp', 'fsdp'))  74.4 us
    gather x1, local copies, waits for them, and re-layouts, per_device(): weight = jnp.take(gathered, inverse, axis=0)  24.8 us
    mul x2, other arithmetic, branch_tail(): kernel[offset] * padded[:, offset:offset + length, :]  16.3 us
  transfers between devices with their start and end apart: 4, of which 4 were waited for; matrix products, arithmetic and copies ran while one was open for 5% of the time, Pallas kernels for 0%

commit v1 on v0

--- a/solution.py
+++ b/solution.py
@@ -2,6 +2,7 @@
 import jax.numpy as jnp
 from jax import lax
 from jax.sharding import PartitionSpec as P
+from jax.lax import all_to_all, psum
 
 EPSILON = 1e-05
 
@@ -42,7 +43,15 @@
     frames_wide = frames.astype(jnp.float32)
     normed, head_back = jax.vjp(norm_rows, frames_wide, gain_in)
     normed_flat = normed.astype(jnp.bfloat16).reshape(token_rows, features)
-    gathered = lax.all_gather(weight_slots, "fsdp", axis=0, tiled=True)
+    gathered = jnp.concatenate(
+        all_to_all(
+            jnp.stack([weight_slots for _ in range(psum(1, "fsdp"))]),
+            "fsdp",
+            split_axis=0,
+            concat_axis=0,
+        ),
+        axis=0,
+    )
     inverse = (
         jnp.zeros((features,), jnp.int32)
         .at[jnp.where(valid_slot, owner_rows, features)]

time: 747 us -> 776 us (1.039)
  waiting for transfers between devices: 522 us -> 534 us
  local copies, waits for them, and re-layouts: 49.9 us -> 58.4 us
    all_to_all x0 -> x1, waiting for transfers between devices: none -> 158 us  [per_device(): all_to_all(jnp.stack([weight_slots for _ in range(psum(1, 'fsdp'))]), 'fs...]
    psum x1, waiting for transfers between devices: 175 us -> 63.5 us  [per_device(): lax.psum((gain_in_grad, gain_mid_grad, kernel_grad), ('dp', 'fsdp'))]
    all_gather x1 -> x0, waiting for transfers between devices: 86.9 us -> none  [per_device(): gathered = lax.all_gather(weight_slots, 'fsdp', axis=0, tiled=True)]
    reduce_scatter x1, waiting for transfers between devices: 120 us -> 174 us  [per_device(): lax.psum_scatter(lax.dot_general(jnp.take(normed_flat, safe_rows, axis=1)...]
    another operation x0 -> x1, local copies, waits for them, and re-layouts: none -> 8.1 us  [per_device(): jnp.stack([weight_slots for _ in range(psum(1, 'fsdp'))])]
  transfers between devices with their start and end apart: 4 -> 4, of which waited for: 4 -> 4; matrix products, arithmetic and copies ran while one was open for 5% -> 4% of each run, Pallas kernels for 0% -> 0%
where the time goes in v1:
time: 776 us
  waiting for transfers between devices  534 us (69%)
  blocking collectives  74.5 us (10%)
  other arithmetic  62.2 us (8%)
  local copies, waits for them, and re-layouts  58.4 us (8%)
  matrix products  21.9 us (3%)
  between operations  16.8 us (2%)
    reduce_scatter x1, waiting for transfers between devices, per_device(): lax.psum_scatter(lax.dot_general(jnp.take(normed_flat, safe_rows, axis=1)...  174 us
    all_to_all x1, waiting for transfers between devices, per_device(): all_to_all(jnp.stack([weight_slots for _ in range(psum(1, 'fsdp'))]), 'fs...  158 us
    psum x1, waiting for transfers between devices, per_device(): weight_sum = lax.psum(owned_rows, 'dp').astype(jnp.float32)  139 us
    psum x1, blocking collectives, per_device(): lax.psum((gain_in_grad, gain_mid_grad, kernel_grad), ('dp', 'fsdp'))  74.5 us
    psum x1, waiting for transfers between devices, per_device(): lax.psum((gain_in_grad, gain_mid_grad, kernel_grad), ('dp', 'fsdp'))  63.5 us
    gather x1, local copies, waits for them, and re-layouts, per_device(): weight = jnp.take(gathered, inverse, axis=0)  24.8 us
    mul x2, other arithmetic, branch_tail(): kernel[offset] * padded[:, offset:offset + length, :]  17 us
  transfers between devices with their start and end apart: 4, of which 4 were waited for; matrix products, arithmetic and copies ran while one was open for 4% of the time, Pallas kernels for 0%

profile of v1, /device:TPU:2, one launch (start us, length us, event | category | flops | bytes accessed | tf_op | source)
XLA Modules:
  0.0 775.7 jit_solution(12847037711735757416)
XLA Ops:
  8.0 8.1 %stack.2 = bf16[16,144,3072]{2,1,0:T(8,128)(2,1)} broadcast(bf16[144,3072]{1,0:T(8,128)(2,1)} %param.11), dimensions={1,2} | broadcast | bytes 15040512 | tf_op jit(solution)/shard_map/stack | solution.py:48
  16.1 7.6 all-to-all-start
  26.5 7.4 gather_fusion.1
  33.9 9.0 %scatter_custom_fusion = s32[1536]{0:T(1024)S(1)} fusion(s32[2304]{0:T(1024)S(1)} %get-tuple-element.117, s32[2304]{0:T(1024)S(1)} %iota.9, s32[]{:T(128)} %constant.48.clone.1), kind=kCustom, calls=%fused_computation.195 | custom fusion | bytes 6148 | tf_op jit(solution)/shard_map/scatter | solution.py:58
  44.1 158.0 %all-to-all-done = bf16[16,144,3072]{2,1,0:T(8,128)(2,1)} async-done(((bf16[16,144,3072]{2,1,0:T(8,128)(2,1)}), bf16[16,144,3072]{2,1,0:T(8,128)(2,1)}, u32[]{:S(2)}, u32[]{:S(2)}) %all-to-all-start) | async-done | bytes 14155808 | tf_op jit(solution)/shard_map/all_to_all | solution.py:47
  202.2 24.8 %gather_fusion = bf16[1536,3072]{1,0:T(8,128)(2,1)} fusion(bf16[2304,3072]{1,0:T(8,128)(2,1)} %bitcast.1, s32[2048]{0:T(1024)S(1)} %pad_clamp_fusion.1), kind=kCustom, calls=%fused_computation | custom fusion | bytes 18880512 | tf_op jit(solution)/shard_map/jit(_take)/gather | solution.py:60
  227.0 6.4 convolution_bitcast_fusion
  233.8 1.2 copy-done.2
  235.0 8.1 %fusion.44 = (f32[256]{0:T(256)S(1)}, f32[1,256,1536]{2,1,0:T(8,128)S(1)}) fusion(f32[1536]{0:T(1024)S(1)} %get-tuple-element.41, f32[1536]{0:T(1024)S(1)} %get-tuple-element.71, f32[1536]{0:T(1024)S(1)} %get-tuple-element.72, f32[1536]{0:T(1024)S(1)} %get-tuple-element.42, f32[1536]{0:T(1024)S(1)} %get-tuple-element.43, f32[1536]{0:T(1024)S(1)} %get-tuple-element.44, ...), kind=kLoop, calls=%fused_computation.216 | loop fusion | flops 25165568 | bytes 3343360 | tf_op jit(solution)/shard_map/jvp()/reduce_sum | solution.py:11
  244.3 1.2 multiply_reduce_fusion.32
  246.6 4.2 multiply_reduce_fusion.30
  250.8 9.8 %broadcast_multiply_fusion.31 = (f32[1,256,1536]{2,1,0:T(8,128)}, f32[1,256,1536]{2,1,0:T(8,128)}, f32[1,256,1536]{2,1,0:T(8,128)}, f32[1,256,1536]{2,1,0:T(8,12...) fusion(f32[1536]{0:T(1024)S(1)} %get-tuple-element.41, ...), kind=kLoop, calls=%fused_computation.149 | loop fusion | flops 7077888 | bytes 28417024 | tf_op jit(solution)/shard_map/transpose(jvp())/mul | solution.py:30
  260.7 7.2 broadcast_multiply_fusion
  267.9 14.8 %pad_add_fusion = f32[1,287,1536]{2,1,0:T(8,128)S(1)} fusion(f32[1,256,1536]{2,1,0:T(8,128)} %get-tuple-element.86, f32[1,256,1536]{2,1,0:T(8,128)} %get-tuple-element.87, f32[1,256,1536]{2,1,0:T(8,128)} %get-tuple-element.88, f32[1,256,1536]{2,1,0:T(8,128)} %get-tuple-element.89, f32[1,256,1536]{2,1,0:T(8,128)} %get-tuple-element.90, ...), kind=kLoop, calls=%fused_computation.24 | loop fusion | flops 11020800 | bytes 42657792 | tf_op jit(solution)/shard_map/transpose(jvp())/add_any | solution.py:30
  282.7 5.4 fusion.16
  290.2 7.9 %convolution_convert_fusion = bf16[2304,3072]{1,0:T(8,128)(2,1)} fusion(bf16[2304,256]{1,0:T(8,128)(2,1)S(1)} %copy-done.6, pred[2304]{0:T(1024)(128)(4,1)S(1)} %copy-done.14, bf16[2304]{0:T(1024)(128)(2,1)S(1)} %get-tuple-element.114, f32[1,256,1536]{2,1,0:T(8,128)S(1)} %fusion.40, f32[1,256,1536]{2,1,0:T(8,128)S(1)} %get-tuple-element.75), kind=kOutput, calls=%fused_computation.3 | convolution fusion | flops 3633709056 | bytes 18488064 | tf_op jit(solution)/shard_map/dot_general | solution.py:77
  298.2 5.1 multiply_reduce_fusion.31
  304.8 7.6 fusion.15
  312.5 173.9 %reduce-scatter.2.cloned.1.call-done = bf16[144,3072]{1,0:T(8,128)(2,1)} async-done(((bf16[2304,3072]{1,0:T(8,128)(2,1)}), bf16[144,3072]{1,0:T(8,128)(2,1)}) %reduce-scatter.2.cloned.1.call-update) | async-done | bytes 884752 | tf_op jit(solution)/shard_map/reduce_scatter | solution.py:76
  487.2 74.5 %all-reduce.67 = (f32[1536]{0:T(1024)}, f32[1536]{0:T(1024)}) all-reduce(f32[1536]{0:T(1024)S(1)} %get-tuple-element.39, f32[1536]{0:T(1024)S(1)} %get-tuple-element.37), channel_id=1, replica_groups=mesh['dp'=16,'fsdp'=16] {'dp','fsdp'}, use_global_device_ids=true, to_apply=%region_12.13 | all-reduce | flops 3072 | bytes 24576 | tf_op jit(solution)/shard_map/psum | solution.py:88
  561.8 1.5 fusion.13
  563.2 63.5 %all-reduce.73.cloned.1.call-done = f32[32,1536]{1,0:T(8,128)} async-done(((f32[32,1536]{1,0:T(8,128)}), f32[32,1536]{1,0:T(8,128)}) %all-reduce.73.cloned.1.call-update) | async-done | bytes 196624 | tf_op jit(solution)/shard_map/psum | solution.py:88
  626.7 138.7 %all-reduce.71.cloned.1.call-done = bf16[144,3072]{1,0:T(8,128)(2,1)} async-done(((bf16[144,3072]{1,0:T(8,128)(2,1)}), bf16[144,3072]{1,0:T(8,128)(2,1)}) %all-reduce.71.cloned.1.call-update) | async-done | bytes 884752 | tf_op jit(solution)/shard_map/psum | solution.py:87
  765.4 2.1 copy.17
  (120 shorter events, 10.8 us)
Async XLA Ops:
  16.1 8.3 %copy-start = (bf16[1,256,1536]{2,1,0:T(8,128)(2,1)S(1)}, bf16[1,256,1536]{2,1,0:T(8,128)(2,1)}, u32[]{:S(2)}) copy-start(bf16[1,256,1536]{2,1,0:T(8,128)(2,1)} %param.8) | copy-start | bytes 2359300
  16.1 186.1 %all-to-all-start = ((bf16[16,144,3072]{2,1,0:T(8,128)(2,1)}), bf16[16,144,3072]{2,1,0:T(8,128)(2,1)}, u32[]{:S(2)}, u32[]{:S(2)}) async-start(bf16[16,144,3072]{2,1,0:T(8,128)(2,1)} %stack.2), calls=%async_computation | async-start | bytes 28311552 | tf_op jit(solution)/shard_map/all_to_all | solution.py:47
  23.7 1.9 copy-start.11
  23.7 462.7 %reduce-scatter.2.cloned.1.call-start = ((), (), s32[]{:S(2)}) async-start(), calls=%async_computation.2 | async-start | bytes 15040512 | tf_op jit(solution)/shard_map/reduce_scatter | solution.py:76
  24.6 1.3 copy-start.17
  26.5 16.5 %copy-start.10 = (f32[32,1536]{1,0:T(8,128)S(1)}, f32[32,1536]{1,0:T(8,128)}, u32[]{:S(2)}) copy-start(f32[32,1536]{1,0:T(8,128)} %param.15) | copy-start | bytes 589828
  42.9 200.6 %copy-start.21 = (f32[256]{0:T(256)}, f32[256]{0:T(256)S(1)}, u32[]{:S(2)}) copy-start(f32[256]{0:T(256)S(1)} %compare_convert_fusion.1) | copy-start | bytes 3076
  43.5 183.5 %copy-start.25 = (pred[1536]{0:T(1024)(128)(4,1)}, pred[1536]{0:T(1024)(128)(4,1)S(1)}, u32[]{:S(2)}) copy-start(pred[1536]{0:T(1024)(128)(4,1)S(1)} %compare_and_fusion.1) | copy-start | bytes 4612
  233.4 1.7 copy-start.2
  250.8 9.8 %copy-start.16 = (f32[256]{0:T(256)S(1)}, f32[256]{0:T(256)}, u32[]{:S(2)}) copy-start(f32[256]{0:T(256)} %copy-done.15) | copy-start | bytes 3076
  267.8 14.8 %copy-start.3 = (f32[1,256,3072]{2,1,0:T(8,128)S(1)}, f32[1,256,3072]{2,1,0:T(8,128)}, u32[]{:S(2)}) copy-start(f32[1,256,3072]{2,1,0:T(8,128)} %copy-done.2) | copy-start | bytes 9437188
  267.8 14.8 %copy-start.22 = (f32[256]{0:T(256)S(1)}, f32[256]{0:T(256)}, u32[]{:S(2)}) copy-start(f32[256]{0:T(256)} %copy-done.21) | copy-start | bytes 3076
  288.0 1.2 copy-start.4
  288.0 2.1 copy-start.6
  288.0 2.1 copy-start.14
  298.1 6.6 copy-start.18
  298.2 6.6 copy-start.26
  298.2 328.5 %all-reduce.73.cloned.1.call-start = ((), (), s32[]{:S(2)}) async-start(), calls=%async_computation.4 | async-start | bytes 393216 | tf_op jit(solution)/shard_map/psum | solution.py:88
  304.8 7.7 copy-start.24
  304.8 181.7 %copy-start.20 = (f32[256]{0:T(256)S(1)}, f32[256]{0:T(256)}, u32[]{:S(2)}) copy-start(f32[256]{0:T(256)} %copy-done.19) | copy-start | bytes 3076
  312.4 174.1 %copy-start.1 = (bf16[1,256,1536]{2,1,0:T(8,128)(2,1)S(1)}, bf16[1,256,1536]{2,1,0:T(8,128)(2,1)}, u32[]{:S(2)}) copy-start(bf16[1,256,1536]{2,1,0:T(8,128)(2,1)} %param.8) | copy-start | bytes 2359300
  312.4 453.0 %all-reduce.71.cloned.1.call-start = ((), (), s32[]{:S(2)}) async-start(), calls=%async_computation.3 | async-start | bytes 1769472 | tf_op jit(solution)/shard_map/psum | solution.py:87
  486.4 75.3 %copy-start.8 = (bf16[1,256,1536]{2,1,0:T(8,128)(2,1)S(1)}, bf16[1,256,1536]{2,1,0:T(8,128)(2,1)}, u32[]{:S(2)}) copy-start(bf16[1,256,1536]{2,1,0:T(8,128)(2,1)} %param.9) | copy-start | bytes 2359300
  626.7 140.8 %copy-start.9 = (f32[32,1536]{1,0:T(8,128)S(1)}, f32[32,1536]{1,0:T(8,128)}, u32[]{:S(2)}) copy-start(f32[32,1536]{1,0:T(8,128)} %all-reduce.73.cloned.1.call-done) | copy-start | bytes 589828
  (7 other events, 6.1 us)
Sparse Core Ops, SparseCore 0:
  298.3 188.1 reduce-scatter.1
Sparse Core Ops, SparseCore 1:
  312.5 314.1 all-reduce.72
  629.4 135.9 all-reduce.70
